TPU v7x, 256 devices: a whole 4x4x8 slice. The times are simulated.
256 devices in a mesh: tm: 64 (over x, z, y_lo), tile: 4 (over y_hi, core).
Axes of the slice: x: 4, y: 4 (y_hi: 2, y_lo: 2; y = y_hi * 2 + y_lo), z: 8, core: 2. Of those that a mesh axis runs over, the one named last changes fastest.
Arguments:
- frames: bfloat16 [4096, 8192], P('tm', 'tile')
- partner: int32 [4096], replicated, may hold values from 0 to 4095, as said below
- usable: int32 [4096], replicated, may hold values from 0 to 1, as said below
Outputs:
- cov_inst: float32 [8192, 8192], P('tile', 'tm')
- cov_lag: float32 [8192, 8192], P('tile', 'tm')
Inputs may be any that keep to these rules, and one draw needn't show every extreme that they name: partner[t] is either t itself or a frame of the same trajectory 1 to 16 frames after t; the offset 16 occurs in every draw. usable[t] is 1 only where partner[t] > t.
All inputs are finite; a program needn't handle non-finite values.
Results may differ from a plain program's by a relative error of at most 0.0005.
The roundings to bfloat16 on the way count: a program that leaves them out, or rounds other values in their place, can miss the bound.
Values may be sent and summed in bfloat16 or wider, within the bound.
A program may use at most 64 MiB of HBM per device.

v0:
```python
import jax
import jax.numpy as jnp
from jax import lax
from jax.sharding import PartitionSpec as P


def shards(frames, partner, usable):
    frames_dev, block_width = frames.shape
    tm_count = lax.axis_size("tm")
    tile_count = lax.axis_size("tile")
    column_width = block_width * tile_count // tm_count
    weight = usable.astype(jnp.float32)
    weight_half = usable.astype(jnp.bfloat16)
    frame_count = jnp.sum(weight)
    local_wide = lax.all_gather(frames, "tile", axis=1, tiled=True)
    column = lax.all_to_all(local_wide, "tm", split_axis=1, concat_axis=0, tiled=True)
    lagged = jnp.take(column, partner, axis=0)
    mean_col = (
        jnp.dot(weight_half[None, :], column, preferred_element_type=jnp.float32) / frame_count
    )
    mean_lag = (
        jnp.dot(weight_half[None, :], lagged, preferred_element_type=jnp.float32) / frame_count
    )
    centered_col = (weight[:, None] * (column.astype(jnp.float32) - mean_col)).astype(jnp.bfloat16)
    centered_lag = (weight[:, None] * (lagged.astype(jnp.float32) - mean_lag)).astype(jnp.bfloat16)
    paired = jnp.concatenate([centered_col, centered_lag], axis=1)
    contract_frames = (((0,), (0,)), ((), ()))
    own_weight = lax.dynamic_slice_in_dim(
        weight_half, lax.axis_index("tm") * frames_dev, frames_dev, 0
    )
    local_sum = jnp.dot(own_weight[None, :], frames, preferred_element_type=jnp.float32)
    mean_row = lax.psum(local_sum, "tm") / frame_count
    centered_rows = (
        lax.all_gather(frames, "tm", axis=0, tiled=True).astype(jnp.float32) - mean_row
    ).astype(jnp.bfloat16)
    product = lax.dot_general(
        centered_rows, paired, contract_frames, preferred_element_type=jnp.float32
    )
    scaled = product / frame_count
    return (scaled[:, :column_width], scaled[:, column_width:])


def solution(mesh):
    in_specs = (P("tm", "tile"), P(), P())
    out_specs = (P("tile", "tm"), P("tile", "tm"))
    return jax.shard_map(shards, mesh=mesh, in_specs=in_specs, out_specs=out_specs, check_vma=False)
```

profile of v0, /device:TPU:1, one launch (start us, length us, event | category | flops | bytes accessed | tf_op | source)
XLA Modules:
  0.0 450.6 jit_solution(10919465198756509816)
XLA Ops:
  7.2 0.0 all-gather.5.cloned.1.call-start
  7.2 0.7 all-gather.5.cloned.1.call-update
  7.9 0.0 all-gather.3.cloned.1.call-start
  7.9 0.7 all-gather.3.cloned.1.call-update
  8.6 0.0 copy-start.2
  8.7 0.0 copy-start
  8.7 0.0 copy-start.1
  8.7 28.7 %all-gather.5.cloned.1.call-done = bf16[64,8192]{1,0:T(8,128)(2,1)} async-done(((bf16[64,2048]{1,0:T(8,128)(2,1)}), bf16[64,8192]{1,0:T(8,128)(2,1)}) %all-gather.5.cloned.1.call-update) | async-done | bytes 1048592 | tf_op jit(solution)/shard_map/all_gather | solution.py:15
  37.4 2.5 copy_bitcast_fusion
  39.9 10.2 %all-to-all-start = ((bf16[64,64,128]{2,0,1:T(8,128)(2,1)}), bf16[64,64,128]{2,0,1:T(8,128)(2,1)S(1)}, u32[]{:S(2)}, u32[]{:S(2)}) async-start(bf16[64,64,128]{2,0,1:T(8,128)(2,1)} %copy_bitcast_fusion), calls=%async_computation | async-start | bytes 2097152 | tf_op jit(solution)/shard_map/all_to_all | solution.py:16
  50.1 0.0 copy-done.2
  50.1 0.0 copy-done
  50.1 0.2 fusion.9
  50.3 162.7 %psum.7 = f32[1,2048]{1,0:T(1,128)S(1)} all-reduce(f32[1,2048]{1,0:T(1,128)S(1)} %fusion.9), channel_id=1, replica_groups=mesh['tm'=64,'tile'=4] {'tm'}, use_global_device_ids=true, to_apply=%region_0.0 | all-reduce | flops 2048 | bytes 16384 | tf_op jit(solution)/shard_map/psum | solution.py:32
  213.0 0.6 convert_reduce_fusion
  213.6 0.0 copy-done.1
  213.6 0.7 broadcast_divide_fusion
  214.3 0.0 all-to-all-done
  214.3 12.1 %gather_fusion = bf16[4096,128]{1,0:T(8,128)(2,1)S(1)} fusion(bf16[4096,128]{1,0:T(8,128)(2,1)S(1)} %bitcast.26, s32[4096]{0:T(1024)S(1)} %fusion.8), kind=kCustom, calls=%fused_computation | custom fusion | bytes 2113536 | tf_op jit(solution)/shard_map/jit(_take)/gather | solution.py:17
  226.5 0.9 fusion.6
  227.3 1.4 fusion.7
  228.7 3.8 multiply_convert_fusion.1
  232.5 200.4 %all-gather.3.cloned.1.call-done = bf16[4096,2048]{1,0:T(8,128)(2,1)} async-done(((bf16[64,2048]{1,0:T(8,128)(2,1)}), bf16[4096,2048]{1,0:T(8,128)(2,1)}) %all-gather.3.cloned.1.call-update) | async-done | bytes 16777232 | tf_op jit(solution)/shard_map/all_gather | solution.py:34
  432.9 9.4 %fusion.2 = f32[2048,256]{1,0:T(8,128)S(1)} fusion(bf16[4096,2048]{1,0:T(8,128)(2,1)} %all-gather.3.cloned.1.call-done, f32[2048]{0:T(1024)S(1)} %bitcast.28, bf16[4096,128]{1,0:T(8,128)(2,1)} %get-tuple-element.5, bf16[4096,128]{1,0:T(8,128)(2,1)S(1)} %get-tuple-element.4, f32[]{:T(128)} %convert_reduce_fusion), kind=kOutput, calls=%fused_computation.4 | convolution fusion | flops 4324851712 | bytes 20979716 | tf_op jit(solution)/shard_map/dot_general | solution.py:36
  442.3 1.5 fusion.14
  (4 shorter events, 0.0 us)
Async XLA Ops:
  7.2 30.2 %all-gather.5.cloned.1.call-start = ((), (), s32[]{:S(2)}) async-start(), calls=%async_computation.2 | async-start | bytes 1310720 | tf_op jit(solution)/shard_map/all_gather | solution.py:15
  7.9 425.0 %all-gather.3.cloned.1.call-start = ((), (), s32[]{:S(2)}) async-start(), calls=%async_computation.1 | async-start | bytes 17039360 | tf_op jit(solution)/shard_map/all_gather | solution.py:34
  8.6 41.4 %copy-start.2 = (s32[4096]{0:T(1024)S(1)}, s32[4096]{0:T(1024)}, u32[]{:S(2)}) copy-start(s32[4096]{0:T(1024)} %param.5) | copy-start | bytes 49156
  8.7 41.5 %copy-start = (bf16[64,2048]{1,0:T(8,128)(2,1)S(1)}, bf16[64,2048]{1,0:T(8,128)(2,1)}, u32[]{:S(2)}) copy-start(bf16[64,2048]{1,0:T(8,128)(2,1)} %param.3) | copy-start | bytes 786436
  8.7 204.9 %copy-start.1 = (s32[4096]{0:T(1024)S(1)}, s32[4096]{0:T(1024)}, u32[]{:S(2)}) copy-start(s32[4096]{0:T(1024)} %param.4) | copy-start | bytes 49156
  39.9 174.4 %all-to-all-start = ((bf16[64,64,128]{2,0,1:T(8,128)(2,1)}), bf16[64,64,128]{2,0,1:T(8,128)(2,1)S(1)}, u32[]{:S(2)}, u32[]{:S(2)}) async-start(bf16[64,64,128]{2,0,1:T(8,128)(2,1)} %copy_bitcast_fusion), calls=%async_computation | async-start | bytes 2097152 | tf_op jit(solution)/shard_map/all_to_all | solution.py:16
Sparse Core Ops, SparseCore 0:
  9.8 27.5 all-gather.4
  39.2 393.6 all-gather.2
where the time goes:
time: 451 us
  waiting for transfers between devices  230 us (51%)
  blocking collectives  163 us (36%)
  local copies, waits for them, and re-layouts  16.1 us (4%)
  between operations  14.2 us (3%)
  matrix products  11.9 us (3%)
  starting transfers between devices  10.3 us (2%)
  other arithmetic  5.07 us (1%)
    all_gather x1, waiting for transfers between devices, shards(): lax.all_gather(frames, 'tm', axis=0, tiled=True).astype(jnp.float32)  200 us
    psum x1, blocking collectives, shards(): mean_row = lax.psum(local_sum, 'tm') / frame_count  163 us
    all_gather x1, waiting for transfers between devices, shards(): local_wide = lax.all_gather(frames, 'tile', axis=1, tiled=True)  28.7 us
    gather x1, local copies, waits for them, and re-layouts, shards(): lagged = jnp.take(column, partner, axis=0)  12.1 us
    all_to_all x1, starting transfers between devices, shards(): lax.all_to_all(local_wide, 'tm', split_axis=1, concat_axis=0, tiled=True)  10.2 us
    dot_general x1, matrix products, shards(): lax.dot_general(centered_rows, paired, contract_frames, preferred_element...  9.38 us
  transfers between devices with their start and end apart: 3, of which 2 were waited for; matrix products, arithmetic and copies ran while one was open for 5% of the time, Pallas kernels for 0%

commit v1 on v0

v1 whole, which is shorter than its diff:
```python
import jax
import jax.numpy as jnp
from jax import lax
from jax.experimental import pallas as pl
from jax.experimental.pallas import tpu as pltpu
from jax.sharding import PartitionSpec as P

MESH = pl.DeviceIdType.MESH
NX, NZ, NL = 4, 8, 2
CHUNKS = 4
W = 128


def coords():
    tm, tile = lax.axis_index("tm"), lax.axis_index("tile")
    return tm // (NZ * NL), (tm // NL) % NZ, tm % NL, tile // 2, tile % 2


def device(x, z, yl, yh, c):
    return (x * (NZ * NL) + z * NL + yl, yh * 2 + c)


def kernel(
    partner_ref, usable_ref, frames_ref, inst_ref, lag_ref,
    row, ul, rt, wcol, outb, stat,
    ra_s, ra_r, ca_s, ca_r, own_sem, ring_s, ring_r, cx_s, cx_r, cy_s, cy_r, cc_s, cc_r, out_s, out_r, keep_sem,
):
    x, z, yl, yh, c = coords()
    tile = yh * 2 + c
    nblk = NX * NZ

    peers = []
    for dx in range(NX):
        for dy in range(NL):
            if dx or dy:
                peers.append(device((x + dx) % NX, z, (yl + dy) % NL, yh, c))
    for dz in range(1, NZ):
        for dy in range(NL):
            peers.append(device(x, (z + dz) % NZ, (yl + dy) % NL, yh, c))
    peers.append(device(x, z, yl, 1 - yh, c))
    peers.append(device(x, z, yl, yh, 1 - c))
    barrier = pltpu.get_barrier_semaphore()
    for p in peers:
        pl.semaphore_signal(barrier, inc=1, device_id=p, device_id_type=MESH)

    own_row = pltpu.make_async_copy(
        frames_ref.at[:, pl.ds(pl.multiple_of(x * 512, 512), 512)],
        row.at[x, z, pl.ds(pl.multiple_of(yl * 64, 64), 64), :], own_sem.at[0])
    own_row.start()

    def col_piece(t, start, size):
        return ul.at[pl.ds(start, size), pl.ds(pl.multiple_of(t * W, W), W)]

    my_block = z * NL + yl
    own_col = pltpu.make_async_copy(
        frames_ref.at[:, pl.ds(pl.multiple_of(my_block * W, W), W)],
        col_piece(tile, pl.multiple_of(x * 1024 + my_block * 64, 64), 64), own_sem.at[1])
    own_col.start()

    pl.semaphore_wait(barrier, len(peers))

    row_a2a = []
    for dx in range(NX):
        for dy in range(NL):
            if dx or dy:
                k = dx * NL + dy
                tx = (x + dx) % NX
                cp = pltpu.make_async_remote_copy(
                    src_ref=frames_ref.at[:, pl.ds(pl.multiple_of(tx * 512, 512), 512)],
                    dst_ref=row.at[x, z, pl.ds(pl.multiple_of(yl * 64, 64), 64), :],
                    send_sem=ra_s.at[k], recv_sem=ra_r.at[k],
                    device_id=device(tx, z, (yl + dy) % NL, yh, c), device_id_type=MESH)
                cp.start()
                row_a2a.append(cp)
    col_a2a = []
    for dz in range(NZ):
        for dy in range(NL):
            if dz or dy:
                k = dz * NL + dy
                tz, ty = (z + dz) % NZ, (yl + dy) % NL
                cp = pltpu.make_async_remote_copy(
                    src_ref=frames_ref.at[:, pl.ds(pl.multiple_of((tz * NL + ty) * W, W), W)],
                    dst_ref=col_piece(tile, pl.multiple_of(x * 1024 + my_block * 64, 64), 64),
                    send_sem=ca_s.at[k], recv_sem=ca_r.at[k],
                    device_id=device(x, tz, ty, yh, c), device_id_type=MESH)
                cp.start()
                col_a2a.append(cp)

    total = jnp.sum(usable_ref[...].astype(jnp.float32))

    def weights(i, _):
        w = usable_ref[pl.ds(i, 1), :].astype(jnp.float32)
        wcol[pl.ds(pl.multiple_of(i * W, W), W), :] = jnp.broadcast_to(w, (W, W)).T
        return 0

    lax.fori_loop(0, nblk, weights, 0)
    ul[pl.ds(4096, W), :] = jnp.zeros((W, 1024), jnp.bfloat16)

    def ring(j, d, h):
        step = 1 if d == 0 else NZ - 1
        blk = (z + (NZ - step) * (h - 1)) % NZ
        ref = row.at[:, blk, :, pl.ds(j * W, W)]
        return pltpu.make_async_remote_copy(
            src_ref=ref, dst_ref=ref, send_sem=ring_s.at[d, j, h - 1], recv_sem=ring_r.at[d, j, h - 1],
            device_id=device(x, (z + step) % NZ, yl, yh, c), device_id_type=MESH)

    def hops(j, d):
        return 4 if j % 2 == d else 3

    own_row.wait()
    for cp in row_a2a:
        cp.wait_recv()
    for j in (0, 1):
        for d in (0, 1):
            ring(j, d, 1).start()

    def ring_step(j, h):
        for d in (0, 1):
            if h <= hops(j, d):
                ring(j, d, h).wait_recv()
                if h < hops(j, d):
                    ring(j, d, h + 1).start()

    def frames_of(k):
        return pl.multiple_of(((x + NX - k) % NX) * 1024, 1024)

    def col_x(dx):
        ref = col_piece(tile, frames_of(0), 1024)
        return pltpu.make_async_remote_copy(
            src_ref=ref, dst_ref=ref, send_sem=cx_s.at[dx], recv_sem=cx_r.at[dx],
            device_id=device((x + dx) % NX, z, yl, yh, c), device_id_type=MESH)

    def col_y(k):
        ref = col_piece(tile, frames_of(k), 1024)
        return pltpu.make_async_remote_copy(
            src_ref=ref, dst_ref=ref, send_sem=cy_s.at[k], recv_sem=cy_r.at[k],
            device_id=device(x, z, yl, 1 - yh, c), device_id_type=MESH)

    def col_c(k, other):
        ref = col_piece(tile if other == 0 else (1 - yh) * 2 + c, frames_of(k), 1024)
        return pltpu.make_async_remote_copy(
            src_ref=ref, dst_ref=ref, send_sem=cc_s.at[other, k], recv_sem=cc_r.at[other, k],
            device_id=device(x, z, yl, yh, 1 - c), device_id_type=MESH)

    own_col.wait()
    for cp in col_a2a:
        cp.wait_recv()
    for dx in (1, 3, 2):
        col_x(dx).start()
    col_y(0).start()
    col_c(0, 0).start()

    def from_x(k):
        col_x(k).wait_recv()
        col_y(k).start()
        col_c(k, 0).start()

    def from_y(k):
        col_y(k).wait_recv()
        col_c(k, 1).start()

    def lag_blocks(lo, hi):
        def body(i, acc):
            base = pl.multiple_of(i * W, W)
            p = partner_ref[pl.ds(i, 1), :] - base
            s = lax.broadcasted_iota(jnp.int32, (2 * W, W), 0)
            pick = jnp.where(s == p, 1.0, 0.0).astype(jnp.bfloat16)
            raw = ul[pl.ds(base, 2 * W), pl.ds(0, 512)]
            lagged = lax.dot_general(pick, raw, (((0,), (0,)), ((), ())), preferred_element_type=jnp.float32)
            ul[pl.ds(base, W), pl.ds(512, 512)] = lagged.astype(jnp.bfloat16)
            w = wcol[pl.ds(base, W), :]
            now = raw[:W].astype(jnp.float32)
            parts = [now[:, k * W:(k + 1) * W] * w for k in range(4)]
            parts += [lagged[:, k * W:(k + 1) * W] * w for k in range(4)]
            prod = jnp.concatenate(parts, axis=1)
            return acc + jnp.sum(prod.reshape(16, 8, 1024), axis=0)

        stat[...] += lax.fori_loop(lo, hi, body, jnp.zeros((8, 1024), jnp.float32))

    def center_blocks(lo, hi, mean):
        def body(i, _):
            sl = pl.ds(pl.multiple_of(i * W, W), W)
            ul[sl, :] = (ul[sl, :].astype(jnp.float32) - mean).astype(jnp.bfloat16)
            return 0

        lax.fori_loop(lo, hi, body, 0)

    def out_copy(j, w, dx):
        tx = (x + dx) % NX
        dst = (inst_ref if w == 0 else lag_ref).at[pl.ds(pl.multiple_of(x * 512 + j * W, W), W), :]
        if dx == 0:
            return pltpu.make_async_copy(outb.at[j, w, tx], dst, keep_sem.at[j, w])
        return pltpu.make_async_remote_copy(
            src_ref=outb.at[j, w, tx], dst_ref=dst, send_sem=out_s.at[j, w, dx], recv_sem=out_r.at[j, w, dx],
            device_id=device(tx, z, yl, yh, c), device_id_type=MESH)

    def chunk(j):
        def sums(i, acc):
            v = row[i // NZ, i % NZ, :, j * W:(j + 1) * W].astype(jnp.float32)
            v = v * wcol[pl.ds(pl.multiple_of(i * W, W), W), :]
            return acc + jnp.sum(v.reshape(16, 8, W), axis=0)

        acc = lax.fori_loop(0, nblk, sums, jnp.zeros((8, W), jnp.float32))
        mean = jnp.sum(acc, axis=0, keepdims=True) / total

        def turn(i, _):
            sl = pl.ds(pl.multiple_of(i * W, W), W)
            v = row[i // NZ, i % NZ, :, j * W:(j + 1) * W].astype(jnp.float32)
            v = (v - mean) * wcol[sl, :]
            rt[:, sl] = v.T.astype(jnp.bfloat16)
            return 0

        lax.fori_loop(0, nblk, turn, 0)

        def multiply(n, _):
            cols = pl.ds(pl.multiple_of(n * 256, 256), 256)
            prod = jnp.dot(rt[...], ul[pl.ds(0, 4096), cols], preferred_element_type=jnp.float32) / total
            outb[j, n // 2, (n % 2) * 2] = prod[:, :W]
            outb[j, n // 2, (n % 2) * 2 + 1] = prod[:, W:]
            return 0

        lax.fori_loop(0, 4, multiply, 0)
        for dx in (2, 1, 3, 0):
            for w in (0, 1):
                out_copy(j, w, dx).start()

    stat[...] = jnp.zeros_like(stat)
    ring_step(0, 1)
    ring_step(1, 1)
    from_x(1)
    from_x(3)
    ring_step(0, 2)
    ring_step(1, 2)
    from_x(2)
    from_y(0)
    ring_step(0, 3)
    for d in (0, 1):
        ring(2, d, 1).start()
    ring_step(1, 3)
    for d in (0, 1):
        ring(3, d, 1).start()
    for k in (1, 3, 2):
        from_y(k)
    ring_step(0, 4)
    ring_step(1, 4)
    for k in (0, 1, 3, 2):
        col_c(k, 0).wait_recv()
    for k in (0, 1, 3, 2):
        col_c(k, 1).wait_recv()
    ring_step(2, 1)
    lag_blocks(0, 8)
    ring_step(3, 1)
    lag_blocks(8, 16)
    lag_blocks(16, 24)
    ring_step(2, 2)
    lag_blocks(24, 32)
    for dx in (1, 2, 3):
        col_x(dx).wait_send()
    for k in range(4):
        col_y(k).wait_send()
        col_c(k, 0).wait_send()
        col_c(k, 1).wait_send()
    mean = jnp.sum(stat[...], axis=0, keepdims=True) / total
    ring_step(3, 2)
    center_blocks(0, 16, mean)
    ring_step(2, 3)
    center_blocks(16, 32, mean)
    ring_step(3, 3)
    chunk(0)
    ring_step(2, 4)
    chunk(1)
    ring_step(3, 4)
    chunk(2)
    chunk(3)

    for cp in row_a2a + col_a2a:
        cp.wait_send()
    for j in range(CHUNKS):
        for d in (0, 1):
            for h in range(1, hops(j, d) + 1):
                ring(j, d, h).wait_send()
    for j in range(CHUNKS):
        for w in (0, 1):
            for dx in range(NX):
                out_copy(j, w, dx).wait()


def shards(frames, partner, usable):
    dma = pltpu.SemaphoreType.DMA
    out = jax.ShapeDtypeStruct((2048, W), jnp.float32)
    vmem, anywhere = pl.BlockSpec(memory_space=pltpu.VMEM), pl.BlockSpec(memory_space=pl.ANY)
    return pl.pallas_call(
        kernel,
        out_shape=(out, out),
        in_specs=[vmem, vmem, vmem],
        out_specs=(anywhere, anywhere),
        scratch_shapes=[
            pltpu.VMEM((NX, NZ, W, 512), jnp.bfloat16),
            pltpu.VMEM((4096 + W, 1024), jnp.bfloat16),
            pltpu.VMEM((W, 4096), jnp.bfloat16),
            pltpu.VMEM((4096, W), jnp.float32),
            pltpu.VMEM((CHUNKS, 2, NX, W, W), jnp.float32),
            pltpu.VMEM((8, 1024), jnp.float32),
            dma((8,)), dma((8,)), dma((16,)), dma((16,)), dma((2,)),
            dma((2, CHUNKS, 4)), dma((2, CHUNKS, 4)),
            dma((4,)), dma((4,)), dma((4,)), dma((4,)), dma((2, 4)), dma((2, 4)),
            dma((CHUNKS, 2, NX)), dma((CHUNKS, 2, NX)), dma((CHUNKS, 2)),
        ],
        compiler_params=pltpu.CompilerParams(
            collective_id=0, has_side_effects=True, vmem_limit_bytes=48 << 20),
        name="covariances",
    )(partner.reshape(32, W), usable.reshape(32, W), frames)


def solution(mesh):
    in_specs = (P("tm", "tile"), P(), P())
    out_specs = (P("tile", "tm"), P("tile", "tm"))
    return jax.shard_map(shards, mesh=mesh, in_specs=in_specs, out_specs=out_specs, check_vma=False)
```

time: 451 us -> 105 us (0.23)
  waiting for transfers between devices: 230 us -> 0 us
  blocking collectives: 163 us -> 0 us
  Pallas kernels: 0 us -> 99.3 us
  between operations: 14.2 us -> 0.65 us
  matrix products: 11.9 us -> 0 us
  local copies, waits for them, and re-layouts: 16.1 us -> 4.32 us
  starting transfers between devices: 10.3 us -> 0 us
  other arithmetic: 5.07 us -> 0 us
    all_gather x2 -> x0, waiting for transfers between devices: 229 us -> none  [the longest x1 200 us: shards(): lax.all_gather(frames, 'tm', axis=0, tiled=True).astype(jnp.float32)]
    psum x1 -> x0, blocking collectives: 163 us -> none  [shards(): mean_row = lax.psum(local_sum, 'tm') / frame_count]
    pallas_call x0 -> x1, Pallas kernels: none -> 99.3 us  [shards(): pl.pallas_call(kernel, out_shape=(out, out), in_specs=[vmem, vmem, vmem],...]
    gather x1 -> x0, local copies, waits for them, and re-layouts: 12.1 us -> none  [shards(): lagged = jnp.take(column, partner, axis=0)]
    dot_general x4 -> x0, matrix products: 11.9 us -> none  [the longest x1 9.38 us: shards(): lax.dot_general(centered_rows, paired, contract_frames, preferred_element...]
    all_to_all x1 -> x0, starting transfers between devices: 10.2 us -> none  [shards(): lax.all_to_all(local_wide, 'tm', split_axis=1, concat_axis=0, tiled=True)]
  transfers between devices with their start and end apart: 3 -> 0, of which waited for: 2 -> 0; matrix products, arithmetic and copies ran while one was open for 5% -> 0% of each run, Pallas kernels for 0% -> 0%
where the time goes in v1:
time: 105 us; the launch traced here: 104 us
  Pallas kernels  99.3 us (95%)
  local copies, waits for them, and re-layouts  4.32 us (4%)
    pallas_call x1, Pallas kernels, shards(): pl.pallas_call(kernel, out_shape=(out, out), in_specs=[vmem, vmem, vmem],...  99.3 us
    unnamed x8, local copies, waits for them, and re-layouts  4.32 us

profile of v1, /device:TPU:1, one launch (start us, length us, event | category | flops | bytes accessed | tf_op | source)
XLA Modules:
  0.0 104.3 jit_solution(4839216437713733976)
XLA Ops:
  0.6 0.0 copy-start
  0.6 0.9 copy-done
  1.6 0.0 copy-start.1
  1.6 0.7 copy-done.1
  2.3 0.0 copy-start.2
  2.3 0.7 copy-done.2
  3.0 99.3 %covariances.1 = (f32[2048,128]{1,0:T(8,128)S(1)}, f32[2048,128]{1,0:T(8,128)S(1)}) custom-call(s32[32,128]{1,0:T(8,128)S(1)} %bitcast.2, s32[32,128]{1,0:T(8,128)S(1)} %bitcast.3, bf16[64,2048]{1,0:T(8,128)(2,1)S(1)} %copy-done), custom_call_target="tpu_custom_call" | custom-call | tf_op jit(solution)/shard_map/covariances/pallas_call | solution.py:292
  102.3 1.0 copy.7
  103.3 1.0 copy.8
Async XLA Ops:
  0.6 1.0 copy-start
  1.6 0.7 copy-start.1
  2.3 0.7 copy-start.2

commit v2 on v0

v2 whole, which is shorter than its diff:
```python
import jax
import jax.numpy as jnp
from jax import lax
from jax.experimental import pallas as pl
from jax.experimental.pallas import tpu as pltpu
from jax.sharding import PartitionSpec as P

MESH = pl.DeviceIdType.MESH
NX, NZ, NL = 4, 8, 2
W = 128
BLOCKS = NX * NZ
FRAMES = BLOCKS * W
CONTRACT_FRAMES = (((0,), (0,)), ((), ()))
B, A0, A1A, A1B = range(4)
HOPS = ((4, 3), (3, 4), (4, 3), (3, 4))


def coords():
    tm, tile = lax.axis_index("tm"), lax.axis_index("tile")
    return tm // (NZ * NL), (tm // NL) % NZ, tm % NL, tile // 2, tile % 2


def device(x, z, yl, yh, c):
    return (x * (NZ * NL) + z * NL + yl, yh * 2 + c)


def at(index, size):
    return pl.ds(pl.multiple_of(index * size, size), size)


def kernel(
    partner_hbm, usable_hbm, frames_hbm, inst_ref, lag_ref,
    partner_ref, usable_ref, frames_ref, row, rc, cn, ul, pick, wcol, outb, stat,
    in_sem, own_sem, rb_s, rb_r, ra_s, ra_r, ca_s, ca_r, ring_s, ring_r, fy_s, fy_r,
    cy_s, cy_r, cx_s, cx_r, cf_s, cf_r, cc_s, cc_r, out_s, out_r, keep_sem,
):
    x, z, yl, yh, c = coords()
    tile = yh * 2 + c
    other_tile = (1 - yh) * 2 + c

    def remote(src, dst, send, recv, dev):
        return pltpu.make_async_remote_copy(
            src_ref=src, dst_ref=dst, send_sem=send, recv_sem=recv, device_id=dev, device_id_type=MESH)

    fetch = [
        pltpu.make_async_copy(frames_hbm, frames_ref, in_sem.at[0]),
        pltpu.make_async_copy(usable_hbm, usable_ref, in_sem.at[1]),
        pltpu.make_async_copy(partner_hbm, partner_ref, in_sem.at[2]),
    ]
    for cp in fetch:
        cp.start()
    peers = []
    for dx in range(NX):
        for dy in range(NL):
            if dx or dy:
                peers.append(device((x + dx) % NX, z, (yl + dy) % NL, yh, c))
    for dz in range(1, NZ):
        for dy in range(NL):
            peers.append(device(x, (z + dz) % NZ, (yl + dy) % NL, yh, c))
    peers.append(device(x, z, yl, 1 - yh, c))
    peers.append(device(x, z, yl, yh, 1 - c))
    barrier = pltpu.get_barrier_semaphore()
    for p in peers:
        pl.semaphore_signal(barrier, inc=1, device_id=p, device_id_type=MESH)

    def piece(t, xs):
        return cn.at[at(xs, 1024), at(t, W)]

    my_block = z * NL + yl
    my_rows = row.at[x, z, at(yl, 64), :]
    my_cols = cn.at[at(x * 16 + my_block, 64), at(tile, W)]
    fetch[0].wait()
    own_row = pltpu.make_async_copy(frames_ref.at[:, at(x, 512)], my_rows, own_sem.at[0])
    own_row.start()
    own_col = pltpu.make_async_copy(frames_ref.at[:, at(my_block, W)], my_cols, own_sem.at[1])
    own_col.start()
    pl.semaphore_wait(barrier, len(peers))

    rows_b, rows_a, cols_a = [], [], []
    for dx in range(1, NX):
        tx = (x + dx) % NX
        rows_b.append(remote(
            frames_ref.at[:, at(tx * 2, 256)], row.at[x, z, at(yl, 64), pl.ds(0, 256)],
            rb_s.at[dx], rb_r.at[dx], device(tx, z, yl, yh, c)))
        rows_b[-1].start()
    for dx in range(NX):
        for dy in range(NL):
            if dx or dy:
                tx, k = (x + dx) % NX, dx * NL + dy
                rows_a.append(remote(
                    frames_ref.at[:, at(tx * 2 + 1, 256)], row.at[x, z, at(yl, 64), pl.ds(256, 256)],
                    ra_s.at[k], ra_r.at[k], device(tx, z, (yl + dy) % NL, yh, c)))
                rows_a[-1].start()
    for dz in range(NZ):
        for dy in range(NL):
            if dz or dy:
                tz, ty, k = (z + dz) % NZ, (yl + dy) % NL, dz * NL + dy
                cols_a.append(remote(
                    frames_ref.at[:, at(tz * NL + ty, W)], my_cols,
                    ca_s.at[k], ca_r.at[k], device(x, tz, ty, yh, c)))
                cols_a[-1].start()

    fetch[1].wait()
    fetch[2].wait()
    total = jnp.sum(usable_ref[...].astype(jnp.float32))

    def weights(i, _):
        w = usable_ref[pl.ds(i, 1), :].astype(jnp.float32)
        wcol[at(i, W), :] = jnp.broadcast_to(w, (W, W)).T
        return 0

    lax.fori_loop(0, BLOCKS, weights, 0, unroll=4)

    def picks(i, _):
        p = (partner_ref[pl.ds(i, 1), :] - i * W).astype(jnp.float32)
        p = jnp.broadcast_to(p, (W, W)).T
        s = lax.broadcasted_iota(jnp.int32, (W, 2 * W), 1).astype(jnp.float32)
        pick[at(i, W), :] = jnp.where(s == jnp.concatenate([p, p], axis=1), 1.0, 0.0).astype(jnp.bfloat16)
        return 0

    lax.fori_loop(0, BLOCKS, picks, 0, unroll=2)
    cn[pl.ds(FRAMES, W), :] = jnp.zeros((W, 512), jnp.bfloat16)

    def ring_ref(s, blk):
        if s == B:
            return row.at[:, blk, at(yl, 64), pl.ds(0, 256)]
        if s == A0:
            return row.at[:, blk, :, pl.ds(256, W)]
        return row.at[pl.ds(0 if s == A1A else 2, 2), blk, :, pl.ds(384, W)]

    def ring(s, d, h):
        step = 1 if d == 0 else NZ - 1
        ref = ring_ref(s, (z + (NZ - step) * (h - 1)) % NZ)
        return remote(ref, ref, ring_s.at[d, s, h - 1], ring_r.at[d, s, h - 1], device(x, (z + step) % NZ, yl, yh, c))

    def over_y(d, h):
        step = 1 if d == 0 else NZ - 1
        ref = ring_ref(B, (z + (NZ - step) * h) % NZ)
        return remote(ref, ref, fy_s.at[d, h], fy_r.at[d, h], device(x, z, 1 - yl, yh, c))

    def ring_start(s):
        for d in (0, 1):
            ring(s, d, 1).start()

    def ring_step(s, h):
        for d in (0, 1):
            if h <= HOPS[s][d]:
                ring(s, d, h).wait_recv()
                if h < HOPS[s][d]:
                    ring(s, d, h + 1).start()
                if s == B:
                    over_y(d, h).start()

    def col_y():
        ref = piece(tile, x)
        return remote(ref, ref, cy_s, cy_r, device(x, z, yl, 1 - yh, c))

    def col_x(d, which):
        ref = piece(other_tile if which else tile, x)
        return remote(ref, ref, cx_s.at[d, which], cx_r.at[d, which],
                      device((x + (1 if d == 0 else NX - 1)) % NX, z, yl, yh, c))

    def col_forward(d):
        step = 1 if d == 0 else NX - 1
        ref = piece(other_tile if d else tile, (x + NX - step) % NX)
        return remote(ref, ref, cf_s.at[d], cf_r.at[d], device((x + step) % NX, z, yl, yh, c))

    def col_c(which, k):
        ref = piece(other_tile if which else tile, (x + k) % NX)
        return remote(ref, ref, cc_s.at[which, k], cc_r.at[which, k], device(x, z, yl, yh, 1 - c))

    def col_step_x(d, which):
        col_x(d, which).wait_recv()
        if which == d:
            col_forward(d).start()
        col_c(which, NX - 1 if d == 0 else 1).start()

    def lagged_columns():
        def body(i, acc):
            raw = cn[pl.ds(pl.multiple_of(i * W, W), 2 * W), :]
            lagged = jnp.dot(pick[at(i, W), :], raw, preferred_element_type=jnp.float32)
            ul[at(i, W), pl.ds(512, 512)] = lagged.astype(jnp.bfloat16)
            w = wcol[at(i, W), :]
            now = raw[:W].astype(jnp.float32)
            parts = [now[:, k * W:(k + 1) * W] * w for k in range(4)]
            parts += [lagged[:, k * W:(k + 1) * W] * w for k in range(4)]
            prod = jnp.concatenate(parts, axis=1)
            return acc + jnp.sum(prod.reshape(16, 8, 1024), axis=0)

        stat[...] = lax.fori_loop(0, BLOCKS, body, jnp.zeros((8, 1024), jnp.float32), unroll=2)

    def center_columns():
        mean = jnp.sum(stat[...], axis=0, keepdims=True) / total

        def body(i, _):
            now = cn[at(i, W), :].astype(jnp.float32) - mean[:, :512]
            lagged = ul[at(i, W), pl.ds(512, 512)].astype(jnp.float32) - mean[:, 512:]
            ul[at(i, W), pl.ds(0, 512)] = now.astype(jnp.bfloat16)
            ul[at(i, W), pl.ds(512, 512)] = lagged.astype(jnp.bfloat16)
            return 0

        lax.fori_loop(0, BLOCKS, body, 0)

    def center_rows(start, width):
        reps = width // W

        def spread(i):
            w = wcol[at(i, W), :]
            return jnp.concatenate([w] * reps, axis=1) if reps > 1 else w

        def sums(i, acc):
            v = row[i // NZ, i % NZ, :, start:start + width].astype(jnp.float32) * spread(i)
            return acc + jnp.sum(v.reshape(16, 8, width), axis=0)

        acc = lax.fori_loop(0, BLOCKS, sums, jnp.zeros((8, width), jnp.float32), unroll=4)
        mean = jnp.sum(acc, axis=0, keepdims=True) / total

        def body(i, _):
            v = row[i // NZ, i % NZ, :, start:start + width].astype(jnp.float32)
            rc[at(i, W), start:start + width] = ((v - mean) * spread(i)).astype(jnp.bfloat16)
            return 0

        lax.fori_loop(0, BLOCKS, body, 0, unroll=2)

    def out_copy(j, w, dx):
        tx = (x + dx) % NX
        dst = (inst_ref if w == 0 else lag_ref).at[at(x * 4 + j, W), :]
        if dx == 0:
            return pltpu.make_async_copy(outb.at[j, w, tx], dst, keep_sem.at[j, w])
        return remote(outb.at[j, w, tx], dst, out_s.at[j, w, dx], out_r.at[j, w, dx], device(tx, z, yl, yh, c))

    def multiply(start, width):
        prod = lax.dot_general(
            rc[:, start:start + width], ul[...], CONTRACT_FRAMES, preferred_element_type=jnp.float32) / total
        first = start // W
        for j in range(width // W):
            for w in (0, 1):
                for t in range(4):
                    n = w * 4 + t
                    outb[first + j, w, t] = prod[j * W:(j + 1) * W, n * W:(n + 1) * W]
            for dx in (2, 1, 3, 0):
                for w in (0, 1):
                    out_copy(first + j, w, dx).start()

    own_row.wait()
    for cp in rows_b:
        cp.wait_recv()
    ring_start(B)
    over_y(0, 0).start()
    for cp in rows_a:
        cp.wait_recv()
    ring_start(A0)
    own_col.wait()
    for cp in cols_a:
        cp.wait_recv()
    for d in (0, 1):
        col_x(d, 0).start()
    col_y().start()
    col_c(0, 0).start()

    ring_step(B, 1)
    ring_step(A0, 1)
    col_y().wait_recv()
    for d in (0, 1):
        col_x(d, 1).start()
    col_c(1, 0).start()
    ring_step(B, 2)
    for d in (0, 1):
        col_step_x(d, 0)
    ring_step(A0, 2)
    ring_step(B, 3)
    ring_start(A1A)
    for d in (0, 1):
        col_step_x(d, 1)
    ring_step(A0, 3)
    ring_start(A1B)
    ring_step(B, 4)
    ring_step(A0, 4)
    center_rows(256, W)
    ring_step(A1A, 1)
    ring_step(A1B, 1)
    for d in (0, 1):
        col_forward(d).wait_recv()
        col_c(d, 2).start()
    for k in range(4):
        for which in (0, 1):
            col_c(which, k).wait_recv()
    lagged_columns()
    ring_step(A1A, 2)
    ring_step(A1B, 2)
    center_columns()
    ring_step(A1A, 3)
    ring_step(A1B, 3)
    multiply(256, W)
    ring_step(A1A, 4)
    ring_step(A1B, 4)
    for d, h in [(0, h) for h in range(5)] + [(1, h) for h in range(1, 4)]:
        over_y(d, h).wait_recv()
    center_rows(0, 256)
    multiply(0, 256)
    center_rows(384, W)
    multiply(384, W)

    for cp in rows_b + rows_a + cols_a:
        cp.wait_send()
    for d in (0, 1):
        for s in (B, A0, A1A, A1B):
            for h in range(1, HOPS[s][d] + 1):
                ring(s, d, h).wait_send()
        for h in range(d, HOPS[B][d] + 1):
            over_y(d, h).wait_send()
        for which in (0, 1):
            col_x(d, which).wait_send()
        col_forward(d).wait_send()
    col_y().wait_send()
    for k in range(4):
        for which in (0, 1):
            col_c(which, k).wait_send()
    for j in range(4):
        for w in (0, 1):
            for dx in range(NX):
                out_copy(j, w, dx).wait()


def shards(frames, partner, usable):
    dma = pltpu.SemaphoreType.DMA
    out = jax.ShapeDtypeStruct((2048, W), jnp.float32)
    anywhere = pl.BlockSpec(memory_space=pl.ANY)
    return pl.pallas_call(
        kernel,
        out_shape=(out, out),
        in_specs=[anywhere] * 3,
        out_specs=(anywhere, anywhere),
        scratch_shapes=[
            pltpu.VMEM((BLOCKS, W), jnp.int32),
            pltpu.VMEM((BLOCKS, W), jnp.int32),
            pltpu.VMEM((64, 2048), jnp.bfloat16),
            pltpu.VMEM((NX, NZ, W, 512), jnp.bfloat16),
            pltpu.VMEM((FRAMES, 512), jnp.bfloat16),
            pltpu.VMEM((FRAMES + W, 512), jnp.bfloat16),
            pltpu.VMEM((FRAMES, 1024), jnp.bfloat16),
            pltpu.VMEM((FRAMES, 2 * W), jnp.bfloat16),
            pltpu.VMEM((FRAMES, W), jnp.float32),
            pltpu.VMEM((4, 2, NX, W, W), jnp.float32),
            pltpu.VMEM((8, 1024), jnp.float32),
            dma((3,)), dma((2,)), dma((4,)), dma((4,)), dma((8,)), dma((8,)), dma((16,)), dma((16,)),
            dma((2, 4, 4)), dma((2, 4, 4)), dma((2, 5)), dma((2, 5)),
            dma(()), dma(()), dma((2, 2)), dma((2, 2)), dma((2,)), dma((2,)), dma((2, 4)), dma((2, 4)),
            dma((4, 2, NX)), dma((4, 2, NX)), dma((4, 2)),
        ],
        compiler_params=pltpu.CompilerParams(
            collective_id=0, has_side_effects=True, vmem_limit_bytes=56 << 20),
        name="covariances",
    )(partner.reshape(BLOCKS, W), usable.reshape(BLOCKS, W), frames)


def solution(mesh):
    in_specs = (P("tm", "tile"), P(), P())
    out_specs = (P("tile", "tm"), P("tile", "tm"))
    return jax.shard_map(shards, mesh=mesh, in_specs=in_specs, out_specs=out_specs, check_vma=False)
```

time: 451 us -> 85.4 us (0.19)
  waiting for transfers between devices: 230 us -> 0 us
  blocking collectives: 163 us -> 0 us
  Pallas kernels: 0 us -> 81.3 us
  between operations: 14.2 us -> 0.65 us
  local copies, waits for them, and re-layouts: 16.1 us -> 3.32 us
  matrix products: 11.9 us -> 0 us
  starting transfers between devices: 10.3 us -> 0 us
  other arithmetic: 5.07 us -> 0 us
    all_gather x2 -> x0, waiting for transfers between devices: 229 us -> none  [the longest x1 200 us: shards(): lax.all_gather(frames, 'tm', axis=0, tiled=True).astype(jnp.float32)]
    psum x1 -> x0, blocking collectives: 163 us -> none  [shards(): mean_row = lax.psum(local_sum, 'tm') / frame_count]
    pallas_call x0 -> x1, Pallas kernels: none -> 81.3 us  [shards(): pl.pallas_call(kernel, out_shape=(out, out), in_specs=[anywhere] * 3, out...]
    gather x1 -> x0, local copies, waits for them, and re-layouts: 12.1 us -> none  [shards(): lagged = jnp.take(column, partner, axis=0)]
    dot_general x4 -> x0, matrix products: 11.9 us -> none  [the longest x1 9.38 us: shards(): lax.dot_general(centered_rows, paired, contract_frames, preferred_element...]
    all_to_all x1 -> x0, starting transfers between devices: 10.2 us -> none  [shards(): lax.all_to_all(local_wide, 'tm', split_axis=1, concat_axis=0, tiled=True)]
  transfers between devices with their start and end apart: 3 -> 0, of which waited for: 2 -> 0; matrix products, arithmetic and copies ran while one was open for 5% -> 0% of each run, Pallas kernels for 0% -> 0%
where the time goes in v2:
time: 85.4 us; the launch traced here: 85.3 us
  Pallas kernels  81.3 us (95%)
  local copies, waits for them, and re-layouts  3.32 us (4%)
    pallas_call x1, Pallas kernels, shards(): pl.pallas_call(kernel, out_shape=(out, out), in_specs=[anywhere] * 3, out...  81.3 us
    unnamed x4, local copies, waits for them, and re-layouts  3.32 us

profile of v2, /device:TPU:1, one launch (start us, length us, event | category | flops | bytes accessed | tf_op | source)
XLA Modules:
  0.0 85.3 jit_solution(1954306847832651504)
XLA Ops:
  0.6 81.3 %covariances.1 = (f32[2048,128]{1,0:T(8,128)}, f32[2048,128]{1,0:T(8,128)}) custom-call(s32[32,128]{1,0:T(8,128)} %bitcast.2, s32[32,128]{1,0:T(8,128)} %bitcast.3, bf16[64,2048]{1,0:T(8,128)(2,1)} %frames_hbm.1), custom_call_target="tpu_custom_call" | custom-call | tf_op jit(solution)/shard_map/covariances/pallas_call | solution.py:329
  81.9 0.0 copy-start
  81.9 2.4 %copy.7 = f32[2048,128]{1,0:T(8,128)} copy(f32[2048,128]{1,0:T(8,128)} %get-tuple-element.4) | data formatting | bytes 2097152
  84.3 0.0 copy-done
  84.3 1.0 %copy.8 = f32[2048,128]{1,0:T(8,128)} copy(f32[2048,128]{1,0:T(8,128)S(1)} %copy-done) | data formatting | bytes 2097152
Async XLA Ops:
  81.9 2.4 %copy-start = (f32[2048,128]{1,0:T(8,128)S(1)}, f32[2048,128]{1,0:T(8,128)}, u32[]{:S(2)}) copy-start(f32[2048,128]{1,0:T(8,128)} %get-tuple-element.5) | copy-start | bytes 3145732

commit v3 on v2

--- a/solution.py
+++ b/solution.py
@@ -11,8 +11,10 @@
 BLOCKS = NX * NZ
 FRAMES = BLOCKS * W
 CONTRACT_FRAMES = (((0,), (0,)), ((), ()))
-B, A0, A1A, A1B = range(4)
-HOPS = ((4, 3), (3, 4), (4, 3), (3, 4))
+B, A0, A1 = range(3)
+HOPS = ((4, 3), (3, 4), (4, 4))
+CODE_ROWS = W + 16
+CODE_MAX = 32767.0
 
 
 def coords():
@@ -29,7 +31,7 @@
 
 
 def kernel(
-    partner_hbm, usable_hbm, frames_hbm, inst_ref, lag_ref,
+    partner_hbm, usable_hbm, frames_hbm, out_ref,
     partner_ref, usable_ref, frames_ref, row, rc, cn, ul, pick, wcol, outb, stat,
     in_sem, own_sem, rb_s, rb_r, ra_s, ra_r, ca_s, ca_r, ring_s, ring_r, fy_s, fy_r,
     cy_s, cy_r, cx_s, cx_r, cf_s, cf_r, cc_s, cc_r, out_s, out_r, keep_sem,
@@ -120,17 +122,19 @@
 
     lax.fori_loop(0, BLOCKS, picks, 0, unroll=2)
     cn[pl.ds(FRAMES, W), :] = jnp.zeros((W, 512), jnp.bfloat16)
-
-    def ring_ref(s, blk):
+    stat[...] = jnp.zeros_like(stat)
+
+    def ring_ref(s, blk, half=slice(None)):
         if s == B:
             return row.at[:, blk, at(yl, 64), pl.ds(0, 256)]
         if s == A0:
             return row.at[:, blk, :, pl.ds(256, W)]
-        return row.at[pl.ds(0 if s == A1A else 2, 2), blk, :, pl.ds(384, W)]
+        return row.at[half, blk, :, pl.ds(384, W)]
 
     def ring(s, d, h):
         step = 1 if d == 0 else NZ - 1
-        ref = ring_ref(s, (z + (NZ - step) * (h - 1)) % NZ)
+        half = pl.ds(2 * d, 2) if h == 4 else slice(None)
+        ref = ring_ref(s, (z + (NZ - step) * (h - 1)) % NZ, half)
         return remote(ref, ref, ring_s.at[d, s, h - 1], ring_r.at[d, s, h - 1], device(x, (z + step) % NZ, yl, yh, c))
 
     def over_y(d, h):
@@ -175,7 +179,7 @@
             col_forward(d).start()
         col_c(which, NX - 1 if d == 0 else 1).start()
 
-    def lagged_columns():
+    def lagged_columns(lo, hi):
         def body(i, acc):
             raw = cn[pl.ds(pl.multiple_of(i * W, W), 2 * W), :]
             lagged = jnp.dot(pick[at(i, W), :], raw, preferred_element_type=jnp.float32)
@@ -187,7 +191,7 @@
             prod = jnp.concatenate(parts, axis=1)
             return acc + jnp.sum(prod.reshape(16, 8, 1024), axis=0)
 
-        stat[...] = lax.fori_loop(0, BLOCKS, body, jnp.zeros((8, 1024), jnp.float32), unroll=2)
+        stat[...] += lax.fori_loop(lo, hi, body, jnp.zeros((8, 1024), jnp.float32), unroll=2)
 
     def center_columns():
         mean = jnp.sum(stat[...], axis=0, keepdims=True) / total
@@ -222,25 +226,34 @@
 
         lax.fori_loop(0, BLOCKS, body, 0, unroll=2)
 
-    def out_copy(j, w, dx):
+    def out_copy(j, dx):
         tx = (x + dx) % NX
-        dst = (inst_ref if w == 0 else lag_ref).at[at(x * 4 + j, W), :]
+        dst = out_ref.at[x * 4 + j]
         if dx == 0:
-            return pltpu.make_async_copy(outb.at[j, w, tx], dst, keep_sem.at[j, w])
-        return remote(outb.at[j, w, tx], dst, out_s.at[j, w, dx], out_r.at[j, w, dx], device(tx, z, yl, yh, c))
+            return pltpu.make_async_copy(outb.at[j, tx], dst, keep_sem.at[j])
+        return remote(outb.at[j, tx], dst, out_s.at[j, dx], out_r.at[j, dx], device(tx, z, yl, yh, c))
+
+    def encode(j, t, w, v):
+        size = jnp.abs(v)
+        top = jnp.maximum(jnp.max(jnp.max(size, axis=1, keepdims=True), axis=0, keepdims=True), 1e-37)
+        e = jnp.ceil(jnp.log2(top) + 1e-3)
+        y = v * lax.rsqrt(jnp.maximum(size, 1e-37)) * (jnp.exp2(-0.5 * e) * CODE_MAX)
+        y = y + jnp.where(v < 0, -0.5, 0.5)
+        outb[j, t, w, pl.ds(0, W), :] = y.astype(jnp.int32).astype(jnp.int16)
+        e = jnp.where(total > 0, e, CODE_MAX)
+        outb[j, t, w, pl.ds(W, 16), :] = jnp.broadcast_to(e, (16, W)).astype(jnp.int32).astype(jnp.int16)
 
     def multiply(start, width):
         prod = lax.dot_general(
             rc[:, start:start + width], ul[...], CONTRACT_FRAMES, preferred_element_type=jnp.float32) / total
-        first = start // W
         for j in range(width // W):
-            for w in (0, 1):
-                for t in range(4):
+            for t in range(NX):
+                for w in (0, 1):
                     n = w * 4 + t
-                    outb[first + j, w, t] = prod[j * W:(j + 1) * W, n * W:(n + 1) * W]
+                    encode(start // W + j, t, w, prod[j * W:(j + 1) * W, n * W:(n + 1) * W])
+        for j in range(width // W):
             for dx in (2, 1, 3, 0):
-                for w in (0, 1):
-                    out_copy(first + j, w, dx).start()
+                out_copy(start // W + j, dx).start()
 
     own_row.wait()
     for cp in rows_b:
@@ -265,46 +278,42 @@
         col_x(d, 1).start()
     col_c(1, 0).start()
     ring_step(B, 2)
+    ring_start(A1)
     for d in (0, 1):
         col_step_x(d, 0)
     ring_step(A0, 2)
+    for d in (0, 1):
+        col_step_x(d, 1)
+    ring_step(A1, 1)
     ring_step(B, 3)
-    ring_start(A1A)
-    for d in (0, 1):
-        col_step_x(d, 1)
-    ring_step(A0, 3)
-    ring_start(A1B)
-    ring_step(B, 4)
-    ring_step(A0, 4)
-    center_rows(256, W)
-    ring_step(A1A, 1)
-    ring_step(A1B, 1)
     for d in (0, 1):
         col_forward(d).wait_recv()
         col_c(d, 2).start()
+    ring_step(A0, 3)
     for k in range(4):
         for which in (0, 1):
             col_c(which, k).wait_recv()
-    lagged_columns()
-    ring_step(A1A, 2)
-    ring_step(A1B, 2)
+    ring_step(A1, 2)
+    lagged_columns(0, 16)
+    ring_step(B, 4)
+    ring_step(A0, 4)
+    lagged_columns(16, 32)
+    ring_step(A1, 3)
     center_columns()
-    ring_step(A1A, 3)
-    ring_step(A1B, 3)
+    center_rows(256, W)
     multiply(256, W)
-    ring_step(A1A, 4)
-    ring_step(A1B, 4)
     for d, h in [(0, h) for h in range(5)] + [(1, h) for h in range(1, 4)]:
         over_y(d, h).wait_recv()
     center_rows(0, 256)
     multiply(0, 256)
+    ring_step(A1, 4)
     center_rows(384, W)
     multiply(384, W)
 
     for cp in rows_b + rows_a + cols_a:
         cp.wait_send()
     for d in (0, 1):
-        for s in (B, A0, A1A, A1B):
+        for s in (B, A0, A1):
             for h in range(1, HOPS[s][d] + 1):
                 ring(s, d, h).wait_send()
         for h in range(d, HOPS[B][d] + 1):
@@ -317,20 +326,28 @@
         for which in (0, 1):
             col_c(which, k).wait_send()
     for j in range(4):
-        for w in (0, 1):
-            for dx in range(NX):
-                out_copy(j, w, dx).wait()
+        for dx in range(NX):
+            out_copy(j, dx).wait()
+
+
+def decode(code_ref, inst_ref, lag_ref):
+    for w, ref in enumerate((inst_ref, lag_ref)):
+        for k in range(code_ref.shape[0]):
+            e = code_ref[k, w, W:CODE_ROWS, :].astype(jnp.float32)[:1]
+            root = code_ref[k, w, :W, :].astype(jnp.float32) * (jnp.exp2(0.5 * e) / CODE_MAX)
+            ref[k * W:(k + 1) * W, :] = root * jnp.abs(root)
 
 
 def shards(frames, partner, usable):
     dma = pltpu.SemaphoreType.DMA
-    out = jax.ShapeDtypeStruct((2048, W), jnp.float32)
+    blocks = frames.shape[1] // W
+    out = jax.ShapeDtypeStruct((blocks, 2, CODE_ROWS, W), jnp.int16)
     anywhere = pl.BlockSpec(memory_space=pl.ANY)
-    return pl.pallas_call(
+    coded = pl.pallas_call(
         kernel,
-        out_shape=(out, out),
+        out_shape=out,
         in_specs=[anywhere] * 3,
-        out_specs=(anywhere, anywhere),
+        out_specs=anywhere,
         scratch_shapes=[
             pltpu.VMEM((BLOCKS, W), jnp.int32),
             pltpu.VMEM((BLOCKS, W), jnp.int32),
@@ -341,17 +358,28 @@
             pltpu.VMEM((FRAMES, 1024), jnp.bfloat16),
             pltpu.VMEM((FRAMES, 2 * W), jnp.bfloat16),
             pltpu.VMEM((FRAMES, W), jnp.float32),
-            pltpu.VMEM((4, 2, NX, W, W), jnp.float32),
+            pltpu.VMEM((4, NX, 2, CODE_ROWS, W), jnp.int16),
             pltpu.VMEM((8, 1024), jnp.float32),
             dma((3,)), dma((2,)), dma((4,)), dma((4,)), dma((8,)), dma((8,)), dma((16,)), dma((16,)),
-            dma((2, 4, 4)), dma((2, 4, 4)), dma((2, 5)), dma((2, 5)),
+            dma((2, 3, 4)), dma((2, 3, 4)), dma((2, 5)), dma((2, 5)),
             dma(()), dma(()), dma((2, 2)), dma((2, 2)), dma((2,)), dma((2,)), dma((2, 4)), dma((2, 4)),
-            dma((4, 2, NX)), dma((4, 2, NX)), dma((4, 2)),
+            dma((4, NX)), dma((4, NX)), dma((4,)),
         ],
         compiler_params=pltpu.CompilerParams(
             collective_id=0, has_side_effects=True, vmem_limit_bytes=56 << 20),
         name="covariances",
     )(partner.reshape(BLOCKS, W), usable.reshape(BLOCKS, W), frames)
+    step = blocks // 4
+    result = jax.ShapeDtypeStruct((blocks * W, W), jnp.float32)
+    spec = pl.BlockSpec((step * W, W), lambda i: (i, 0))
+    return pl.pallas_call(
+        decode,
+        grid=(blocks // step,),
+        out_shape=(result, result),
+        in_specs=[pl.BlockSpec((step, 2, CODE_ROWS, W), lambda i: (i, 0, 0, 0))],
+        out_specs=(spec, spec),
+        name="decode",
+    )(coded)
 
 
 def solution(mesh):

time: 85.4 us -> 74.8 us (0.88)
  Pallas kernels: 81.3 us -> 74 us
  local copies, waits for them, and re-layouts: 3.32 us -> 0 us
    pallas_call x1 -> x2, Pallas kernels: 81.3 us -> 74 us  [the longest x1 70.3 us: shards(): pl.pallas_call(kernel, out_shape=out, in_specs=[anywhere] * 3, out_specs=...]
    unnamed x4 -> x0, local copies, waits for them, and re-layouts: 3.32 us -> none
where the time goes in v3:
time: 74.8 us; the launch traced here: 74.6 us
  Pallas kernels  74 us (99%)
    pallas_call x1, Pallas kernels, shards(): pl.pallas_call(kernel, out_shape=out, in_specs=[anywhere] * 3, out_specs=...  70.3 us
    pallas_call x1, Pallas kernels, shards(): pl.pallas_call(decode, grid=(blocks // step,), out_shape=(result, result)...  3.64 us

profile of v3, /device:TPU:1, one launch (start us, length us, event | category | flops | bytes accessed | tf_op | source)
XLA Modules:
  0.0 74.6 jit_solution(1586462553704738196)
XLA Ops:
  0.6 70.3 %covariances.1.code_ref = s16[16,2,144,128]{3,2,1,0:T(8,128)(2,1)} custom-call(s32[32,128]{1,0:T(8,128)} %bitcast.2, s32[32,128]{1,0:T(8,128)} %bitcast.3, bf16[64,2048]{1,0:T(8,128)(2,1)} %frames_hbm.1), custom_call_target="tpu_custom_call" | custom-call | tf_op jit(solution)/shard_map/covariances/pallas_call | solution.py:346
  71.0 3.6 %decode.1 = (f32[2048,128]{1,0:T(8,128)}, f32[2048,128]{1,0:T(8,128)}) custom-call(s16[16,2,144,128]{3,2,1,0:T(8,128)(2,1)} %covariances.1.code_ref), custom_call_target="tpu_custom_call" | custom-call | tf_op jit(solution)/shard_map/decode/pallas_call | solution.py:375

commit v4 on v3

--- a/solution.py
+++ b/solution.py
@@ -8,11 +8,13 @@
 MESH = pl.DeviceIdType.MESH
 NX, NZ, NL = 4, 8, 2
 W = 128
+LAG = 16
 BLOCKS = NX * NZ
 FRAMES = BLOCKS * W
 CONTRACT_FRAMES = (((0,), (0,)), ((), ()))
 B, A0, A1 = range(3)
-HOPS = ((4, 3), (3, 4), (4, 4))
+HOPS = ((4, 3), (3, 4))
+LANES = (pl.ds(0, 256), pl.ds(256, W), pl.ds(384, W))
 CODE_ROWS = W + 16
 CODE_MAX = 32767.0
 
@@ -32,8 +34,8 @@
 
 def kernel(
     partner_hbm, usable_hbm, frames_hbm, out_ref,
-    partner_ref, usable_ref, frames_ref, row, rc, cn, ul, pick, wcol, outb, stat,
-    in_sem, own_sem, rb_s, rb_r, ra_s, ra_r, ca_s, ca_r, ring_s, ring_r, fy_s, fy_r,
+    partner_ref, usable_ref, frames_ref, row, rc, cn, vl, ul, pick, wcol, vcol, outb, vrow, rsum, csum, rmean, cmean,
+    in_sem, own_sem, rb_s, rb_r, ra_s, ra_r, ca_s, ca_r, ring_s, ring_r, a1_s, a1_r, fy_s, fy_r, rs_s, rs_r, cs_s, cs_r,
     cy_s, cy_r, cx_s, cx_r, cf_s, cf_r, cc_s, cc_r, out_s, out_r, keep_sem,
 ):
     x, z, yl, yh, c = coords()
@@ -59,8 +61,11 @@
     for dz in range(1, NZ):
         for dy in range(NL):
             peers.append(device(x, (z + dz) % NZ, (yl + dy) % NL, yh, c))
-    peers.append(device(x, z, yl, 1 - yh, c))
-    peers.append(device(x, z, yl, yh, 1 - c))
+    for dx in range(NX):
+        for dh in range(2):
+            for dc in range(2):
+                if dh or dc:
+                    peers.append(device((x + dx) % NX, z, yl, (yh + dh) % 2, (c + dc) % 2))
     barrier = pltpu.get_barrier_semaphore()
     for p in peers:
         pl.semaphore_signal(barrier, inc=1, device_id=p, device_id_type=MESH)
@@ -106,9 +111,20 @@
     fetch[2].wait()
     total = jnp.sum(usable_ref[...].astype(jnp.float32))
 
+    ahead = partner_ref[...] - (
+        lax.broadcasted_iota(jnp.int32, (BLOCKS, W), 0) * W + lax.broadcasted_iota(jnp.int32, (BLOCKS, W), 1))
+    lane = lax.broadcasted_iota(jnp.int32, (BLOCKS, W), 1)
+    weight = usable_ref[...].astype(jnp.float32)
+    count = jnp.where(ahead == 0, weight, 0.0)
+    for k in range(1, LAG + 1):
+        r = pltpu.roll(jnp.where(ahead == k, weight, 0.0), k, axis=1)
+        count += jnp.where(lane < k, pltpu.roll(r, 1, axis=0), r)
+    vrow[...] = count
+
     def weights(i, _):
         w = usable_ref[pl.ds(i, 1), :].astype(jnp.float32)
         wcol[at(i, W), :] = jnp.broadcast_to(w, (W, W)).T
+        vcol[at(i, W), :] = jnp.broadcast_to(vrow[pl.ds(i, 1), :], (W, W)).T
         return 0
 
     lax.fori_loop(0, BLOCKS, weights, 0, unroll=4)
@@ -121,30 +137,40 @@
         return 0
 
     lax.fori_loop(0, BLOCKS, picks, 0, unroll=2)
-    cn[pl.ds(FRAMES, W), :] = jnp.zeros((W, 512), jnp.bfloat16)
-    stat[...] = jnp.zeros_like(stat)
-
-    def ring_ref(s, blk, half=slice(None)):
+    vl[pl.ds(FRAMES, W), :] = jnp.zeros((W, 512), jnp.bfloat16)
+
+    def behind(d, h):
+        return (z + (NZ - h if d == 0 else h)) % NZ
+
+    def ahead_z(d):
+        return device(x, (z + (1 if d == 0 else NZ - 1)) % NZ, yl, yh, c)
+
+    def ring(s, d, h):
+        frames = at(yl, 64) if s == B else slice(None)
+        ref = row.at[:, behind(d, h - 1), frames, LANES[s]]
+        return remote(ref, ref, ring_s.at[d, s, h - 1], ring_r.at[d, s, h - 1], ahead_z(d))
+
+    def ring_a1(q, d, h):
+        ref = row.at[q, behind(d, h - 1), :, LANES[A1]]
+        return remote(ref, ref, a1_s.at[d, q, h - 1], a1_r.at[d, q, h - 1], ahead_z(d))
+
+    def over_y(d, h):
+        ref = row.at[:, behind(d, h), at(yl, 64), LANES[B]]
+        return remote(ref, ref, fy_s.at[d, h], fy_r.at[d, h], device(x, z, 1 - yl, yh, c))
+
+    def center_rows(s, blk, half=None, only=None):
+        lo = 0 if s == B else s + 1
+        mean = rmean[lo:lo + 1, :]
         if s == B:
-            return row.at[:, blk, at(yl, 64), pl.ds(0, 256)]
-        if s == A0:
-            return row.at[:, blk, :, pl.ds(256, W)]
-        return row.at[half, blk, :, pl.ds(384, W)]
-
-    def ring(s, d, h):
-        step = 1 if d == 0 else NZ - 1
-        half = pl.ds(2 * d, 2) if h == 4 else slice(None)
-        ref = ring_ref(s, (z + (NZ - step) * (h - 1)) % NZ, half)
-        return remote(ref, ref, ring_s.at[d, s, h - 1], ring_r.at[d, s, h - 1], device(x, (z + step) % NZ, yl, yh, c))
-
-    def over_y(d, h):
-        step = 1 if d == 0 else NZ - 1
-        ref = ring_ref(B, (z + (NZ - step) * h) % NZ)
-        return remote(ref, ref, fy_s.at[d, h], fy_r.at[d, h], device(x, z, 1 - yl, yh, c))
-
-    def ring_start(s):
-        for d in (0, 1):
-            ring(s, d, 1).start()
+            mean = jnp.concatenate([mean, rmean[1:2, :]], axis=1)
+        for q in range(NX) if only is None else (only,):
+            base = (q * NZ + blk) * 2
+            frames, inner = (at(base // 2, W), slice(None)) if half is None else (at(base + half, 64), at(half, 64))
+            v = row[q, blk, inner, LANES[s]].astype(jnp.float32)
+            w = wcol[frames, :]
+            if s == B:
+                w = jnp.concatenate([w, w], axis=1)
+            rc[frames, LANES[s]] = ((v - mean) * w).astype(jnp.bfloat16)
 
     def ring_step(s, h):
         for d in (0, 1):
@@ -155,6 +181,34 @@
                 if s == B:
                     over_y(d, h).start()
 
+    def center_step(s, h):
+        for d in (0, 1):
+            if h <= HOPS[s][d]:
+                center_rows(s, behind(d, h), yl if s == B else None)
+
+    def from_y(h):
+        for d in (0, 1):
+            if d <= h <= HOPS[B][d]:
+                over_y(d, h).wait_recv()
+                center_rows(B, behind(d, h), 1 - yl)
+
+    def a1_goes(q, d, h):
+        return h < 4 or q // 2 == d
+
+    def a1_step(h):
+        for q in range(NX):
+            for d in (0, 1):
+                if a1_goes(q, d, h):
+                    ring_a1(q, d, h).wait_recv()
+                    if h < 4 and a1_goes(q, d, h + 1):
+                        ring_a1(q, d, h + 1).start()
+
+    def center_a1(h):
+        for q in range(NX):
+            for d in (0, 1):
+                if a1_goes(q, d, h):
+                    center_rows(A1, behind(d, h), only=q)
+
     def col_y():
         ref = piece(tile, x)
         return remote(ref, ref, cy_s, cy_r, device(x, z, yl, 1 - yh, c))
@@ -173,65 +227,90 @@
         ref = piece(other_tile if which else tile, (x + k) % NX)
         return remote(ref, ref, cc_s.at[which, k], cc_r.at[which, k], device(x, z, yl, yh, 1 - c))
 
-    def col_step_x(d, which):
-        col_x(d, which).wait_recv()
-        if which == d:
-            col_forward(d).start()
-        col_c(which, NX - 1 if d == 0 else 1).start()
+    def col_step_x(which):
+        for d in (0, 1):
+            col_x(d, which).wait_recv()
+            if which == d:
+                col_forward(d).start()
+            col_c(which, NX - 1 if d == 0 else 1).start()
+        for k in (NX - 1, 1):
+            center_columns(other_tile if which else tile, (x + k) % NX)
+
+    def from_core(which, k):
+        col_c(which, k).wait_recv()
+        center_columns((1 - yh if which else yh) * 2 + 1 - c, (x + k) % NX)
+
+    def row_sums():
+        acc = jnp.zeros((8, 512), jnp.float32)
+        for q in range(NX):
+            v = row[q, z, at(yl, 64), :].astype(jnp.float32)
+            w = wcol[at((q * NZ + z) * 2 + yl, 64), :]
+            v = v * jnp.concatenate([w] * 4, axis=1)
+            acc = acc + jnp.sum(v.reshape(8, 8, 512), axis=0)
+        acc = jnp.sum(acc, axis=0, keepdims=True)
+        mine = rsum.at[z, yl]
+        for r in range(4):
+            mine[r:r + 1, :] = acc[:, r * W:(r + 1) * W]
+        mine[4:8, :] = jnp.zeros((4, W), jnp.float32)
+        copies = []
+        for dz in range(NZ):
+            for dy in range(NL):
+                if dz or dy:
+                    copies.append(remote(
+                        mine, mine, rs_s.at[dz, dy], rs_r.at[dz, dy],
+                        device(x, (z + dz) % NZ, (yl + dy) % NL, yh, c)))
+                    copies[-1].start()
+        return copies
+
+    def column_sums():
+        def body(i, acc):
+            k = x * 8 + i
+            v = cn[at(k, W), at(tile, W)].astype(jnp.float32)
+            now, lag = v * wcol[at(k, W), :], v * vcol[at(k, W), :]
+            return acc + jnp.concatenate(
+                [jnp.sum(now.reshape(16, 8, W), axis=0), jnp.sum(lag.reshape(16, 8, W), axis=0)], axis=1)
+
+        acc = lax.fori_loop(0, 8, body, jnp.zeros((8, 2 * W), jnp.float32), unroll=True)
+        acc = jnp.sum(acc, axis=0, keepdims=True)
+        mine = csum.at[tile, x]
+        mine[0:1, :] = acc[:, :W]
+        mine[1:2, :] = acc[:, W:]
+        mine[2:8, :] = jnp.zeros((6, W), jnp.float32)
+        copies = []
+        for dx in range(NX):
+            for dh in range(2):
+                for dc in range(2):
+                    if dx or dh or dc:
+                        copies.append(remote(
+                            mine, mine, cs_s.at[dx, dh * 2 + dc], cs_r.at[dx, dh * 2 + dc],
+                            device((x + dx) % NX, z, yl, (yh + dh) % 2, (c + dc) % 2)))
+                        copies[-1].start()
+        return copies
+
+    def center_columns(t, xs):
+        means = cmean[t]
+        now, lag = means[0:1, :], means[1:2, :]
+        for i in range(8):
+            frames = at(xs * 8 + i, W)
+            v = cn[frames, at(t, W)].astype(jnp.float32)
+            ul[frames, at(t, W)] = (v - now).astype(jnp.bfloat16)
+            vl[frames, at(t, W)] = (v - lag).astype(jnp.bfloat16)
 
     def lagged_columns(lo, hi):
-        def body(i, acc):
-            raw = cn[pl.ds(pl.multiple_of(i * W, W), 2 * W), :]
-            lagged = jnp.dot(pick[at(i, W), :], raw, preferred_element_type=jnp.float32)
-            ul[at(i, W), pl.ds(512, 512)] = lagged.astype(jnp.bfloat16)
-            w = wcol[at(i, W), :]
-            now = raw[:W].astype(jnp.float32)
-            parts = [now[:, k * W:(k + 1) * W] * w for k in range(4)]
-            parts += [lagged[:, k * W:(k + 1) * W] * w for k in range(4)]
-            prod = jnp.concatenate(parts, axis=1)
-            return acc + jnp.sum(prod.reshape(16, 8, 1024), axis=0)
-
-        stat[...] += lax.fori_loop(lo, hi, body, jnp.zeros((8, 1024), jnp.float32), unroll=2)
-
-    def center_columns():
-        mean = jnp.sum(stat[...], axis=0, keepdims=True) / total
-
         def body(i, _):
-            now = cn[at(i, W), :].astype(jnp.float32) - mean[:, :512]
-            lagged = ul[at(i, W), pl.ds(512, 512)].astype(jnp.float32) - mean[:, 512:]
-            ul[at(i, W), pl.ds(0, 512)] = now.astype(jnp.bfloat16)
+            v = vl[pl.ds(pl.multiple_of(i * W, W), 2 * W), :]
+            lagged = jnp.dot(pick[at(i, W), :], v, preferred_element_type=jnp.float32)
             ul[at(i, W), pl.ds(512, 512)] = lagged.astype(jnp.bfloat16)
             return 0
 
-        lax.fori_loop(0, BLOCKS, body, 0)
-
-    def center_rows(start, width):
-        reps = width // W
-
-        def spread(i):
-            w = wcol[at(i, W), :]
-            return jnp.concatenate([w] * reps, axis=1) if reps > 1 else w
-
-        def sums(i, acc):
-            v = row[i // NZ, i % NZ, :, start:start + width].astype(jnp.float32) * spread(i)
-            return acc + jnp.sum(v.reshape(16, 8, width), axis=0)
-
-        acc = lax.fori_loop(0, BLOCKS, sums, jnp.zeros((8, width), jnp.float32), unroll=4)
-        mean = jnp.sum(acc, axis=0, keepdims=True) / total
-
-        def body(i, _):
-            v = row[i // NZ, i % NZ, :, start:start + width].astype(jnp.float32)
-            rc[at(i, W), start:start + width] = ((v - mean) * spread(i)).astype(jnp.bfloat16)
-            return 0
-
-        lax.fori_loop(0, BLOCKS, body, 0, unroll=2)
-
-    def out_copy(j, dx):
+        lax.fori_loop(lo, hi, body, 0, unroll=4)
+
+    def out_copy(j, w, dx):
         tx = (x + dx) % NX
-        dst = out_ref.at[x * 4 + j]
+        dst = out_ref.at[x * 4 + j, w]
         if dx == 0:
-            return pltpu.make_async_copy(outb.at[j, tx], dst, keep_sem.at[j])
-        return remote(outb.at[j, tx], dst, out_s.at[j, dx], out_r.at[j, dx], device(tx, z, yl, yh, c))
+            return pltpu.make_async_copy(outb.at[j, tx, w], dst, keep_sem.at[j, w])
+        return remote(outb.at[j, tx, w], dst, out_s.at[j, w, dx], out_r.at[j, w, dx], device(tx, z, yl, yh, c))
 
     def encode(j, t, w, v):
         size = jnp.abs(v)
@@ -243,79 +322,117 @@
         e = jnp.where(total > 0, e, CODE_MAX)
         outb[j, t, w, pl.ds(W, 16), :] = jnp.broadcast_to(e, (16, W)).astype(jnp.int32).astype(jnp.int16)
 
-    def multiply(start, width):
+    def multiply(s, w):
+        first, chunks = (0, 2) if s == B else (s + 1, 1)
         prod = lax.dot_general(
-            rc[:, start:start + width], ul[...], CONTRACT_FRAMES, preferred_element_type=jnp.float32) / total
-        for j in range(width // W):
+            rc[:, LANES[s]], ul[:, pl.ds(w * 512, 512)], CONTRACT_FRAMES, preferred_element_type=jnp.float32) / total
+        for j in range(chunks):
             for t in range(NX):
-                for w in (0, 1):
-                    n = w * 4 + t
-                    encode(start // W + j, t, w, prod[j * W:(j + 1) * W, n * W:(n + 1) * W])
-        for j in range(width // W):
+                encode(first + j, t, w, prod[j * W:(j + 1) * W, t * W:(t + 1) * W])
+        for j in range(chunks):
             for dx in (2, 1, 3, 0):
-                out_copy(start // W + j, dx).start()
+                out_copy(first + j, w, dx).start()
 
     own_row.wait()
     for cp in rows_b:
         cp.wait_recv()
-    ring_start(B)
+    for d in (0, 1):
+        ring(B, d, 1).start()
     over_y(0, 0).start()
     for cp in rows_a:
         cp.wait_recv()
-    ring_start(A0)
+    row_parts = row_sums()
+    for d in (0, 1):
+        ring(A0, d, 1).start()
     own_col.wait()
     for cp in cols_a:
         cp.wait_recv()
+    col_parts = column_sums()
+    col_y().start()
     for d in (0, 1):
         col_x(d, 0).start()
-    col_y().start()
     col_c(0, 0).start()
 
     ring_step(B, 1)
     ring_step(A0, 1)
+    for cp in row_parts:
+        cp.wait_recv()
+    rmean[...] = jnp.sum(rsum[...].reshape(NZ * NL, 8, W), axis=0) / total
+    center_rows(B, z, yl)
+    center_rows(A0, z)
+    center_rows(A1, z)
     col_y().wait_recv()
     for d in (0, 1):
         col_x(d, 1).start()
     col_c(1, 0).start()
     ring_step(B, 2)
-    ring_start(A1)
-    for d in (0, 1):
-        col_step_x(d, 0)
+    center_step(B, 1)
+    for cp in col_parts:
+        cp.wait_recv()
+    cmean[...] = (csum[:, 0] + csum[:, 1] + csum[:, 2] + csum[:, 3]) / total
+    center_step(A0, 1)
     ring_step(A0, 2)
-    for d in (0, 1):
-        col_step_x(d, 1)
-    ring_step(A1, 1)
+    col_step_x(0)
+    center_columns(tile, x)
+    center_columns(other_tile, x)
+    center_step(B, 2)
     ring_step(B, 3)
+    for q in range(NX):
+        for d in (0, 1):
+            ring_a1(q, d, 1).start()
+    center_step(A0, 2)
+    from_core(0, 0)
+    from_core(1, 0)
+    from_y(0)
+    from_y(1)
+    ring_step(A0, 3)
+    col_step_x(1)
+    center_step(B, 3)
+    center_step(A0, 3)
+    from_core(0, 1)
+    from_core(0, 3)
+    ring_step(B, 4)
+    ring_step(A0, 4)
+    center_step(B, 4)
+    center_step(A0, 4)
+    from_y(2)
     for d in (0, 1):
         col_forward(d).wait_recv()
         col_c(d, 2).start()
-    ring_step(A0, 3)
-    for k in range(4):
-        for which in (0, 1):
-            col_c(which, k).wait_recv()
-    ring_step(A1, 2)
-    lagged_columns(0, 16)
-    ring_step(B, 4)
-    ring_step(A0, 4)
-    lagged_columns(16, 32)
-    ring_step(A1, 3)
-    center_columns()
-    center_rows(256, W)
-    multiply(256, W)
-    for d, h in [(0, h) for h in range(5)] + [(1, h) for h in range(1, 4)]:
-        over_y(d, h).wait_recv()
-    center_rows(0, 256)
-    multiply(0, 256)
-    ring_step(A1, 4)
-    center_rows(384, W)
-    multiply(384, W)
-
-    for cp in rows_b + rows_a + cols_a:
+    for d in (0, 1):
+        center_columns(other_tile if d else tile, (x + 2) % NX)
+    a1_step(1)
+    from_core(1, 1)
+    from_core(1, 3)
+    from_core(0, 2)
+    from_core(1, 2)
+    multiply(A0, 0)
+    a1_step(2)
+    center_a1(1)
+    from_y(3)
+    from_y(4)
+    multiply(B, 0)
+    a1_step(3)
+    lagged_columns(0, 32)
+    center_a1(2)
+    multiply(A0, 1)
+    center_a1(3)
+    a1_step(4)
+    multiply(B, 1)
+    center_a1(4)
+    multiply(A1, 0)
+    multiply(A1, 1)
+
+    for cp in rows_b + rows_a + cols_a + row_parts + col_parts:
         cp.wait_send()
     for d in (0, 1):
-        for s in (B, A0, A1):
+        for s in (B, A0):
             for h in range(1, HOPS[s][d] + 1):
                 ring(s, d, h).wait_send()
+        for q in range(NX):
+            for h in range(1, 5):
+                if a1_goes(q, d, h):
+                    ring_a1(q, d, h).wait_send()
         for h in range(d, HOPS[B][d] + 1):
             over_y(d, h).wait_send()
         for which in (0, 1):
@@ -326,8 +443,9 @@
         for which in (0, 1):
             col_c(which, k).wait_send()
     for j in range(4):
-        for dx in range(NX):
-            out_copy(j, dx).wait()
+        for w in (0, 1):
+            for dx in range(NX):
+                out_copy(j, w, dx).wait()
 
 
 def decode(code_ref, inst_ref, lag_ref):
@@ -354,16 +472,23 @@
             pltpu.VMEM((64, 2048), jnp.bfloat16),
             pltpu.VMEM((NX, NZ, W, 512), jnp.bfloat16),
             pltpu.VMEM((FRAMES, 512), jnp.bfloat16),
+            pltpu.VMEM((FRAMES, 512), jnp.bfloat16),
             pltpu.VMEM((FRAMES + W, 512), jnp.bfloat16),
             pltpu.VMEM((FRAMES, 1024), jnp.bfloat16),
             pltpu.VMEM((FRAMES, 2 * W), jnp.bfloat16),
             pltpu.VMEM((FRAMES, W), jnp.float32),
+            pltpu.VMEM((FRAMES, W), jnp.float32),
             pltpu.VMEM((4, NX, 2, CODE_ROWS, W), jnp.int16),
-            pltpu.VMEM((8, 1024), jnp.float32),
+            pltpu.VMEM((BLOCKS, W), jnp.float32),
+            pltpu.VMEM((NZ, NL, 8, W), jnp.float32),
+            pltpu.VMEM((4, NX, 8, W), jnp.float32),
+            pltpu.VMEM((8, W), jnp.float32),
+            pltpu.VMEM((4, 8, W), jnp.float32),
             dma((3,)), dma((2,)), dma((4,)), dma((4,)), dma((8,)), dma((8,)), dma((16,)), dma((16,)),
-            dma((2, 3, 4)), dma((2, 3, 4)), dma((2, 5)), dma((2, 5)),
+            dma((2, 2, 4)), dma((2, 2, 4)), dma((2, NX, 4)), dma((2, NX, 4)), dma((2, 5)), dma((2, 5)),
+            dma((NZ, NL)), dma((NZ, NL)), dma((NX, 4)), dma((NX, 4)),
             dma(()), dma(()), dma((2, 2)), dma((2, 2)), dma((2,)), dma((2,)), dma((2, 4)), dma((2, 4)),
-            dma((4, NX)), dma((4, NX)), dma((4,)),
+            dma((4, 2, NX)), dma((4, 2, NX)), dma((4, 2)),
         ],
         compiler_params=pltpu.CompilerParams(
             collective_id=0, has_side_effects=True, vmem_limit_bytes=56 << 20),

time: 74.8 us -> 73.2 us (0.979)
  Pallas kernels: 74 us -> 72.4 us
    pallas_call x1, Pallas kernels: 70.3 us -> 68.8 us  [shards(): pl.pallas_call(kernel, out_shape=out, in_specs=[anywhere] * 3, out_specs=...]
where the time goes in v4:
time: 73.2 us; the launch traced here: 73.1 us
  Pallas kernels  72.4 us (99%)
    pallas_call x1, Pallas kernels, shards(): pl.pallas_call(kernel, out_shape=out, in_specs=[anywhere] * 3, out_specs=...  68.8 us
    pallas_call x1, Pallas kernels, shards(): pl.pallas_call(decode, grid=(blocks // step,), out_shape=(result, result)...  3.64 us

profile of v4, /device:TPU:1, one launch (start us, length us, event | category | flops | bytes accessed | tf_op | source)
XLA Modules:
  0.0 73.1 jit_solution(9207799939451250226)
XLA Ops:
  0.6 68.8 %covariances.1.code_ref = s16[16,2,144,128]{3,2,1,0:T(8,128)(2,1)} custom-call(s32[32,128]{1,0:T(8,128)} %bitcast.2, s32[32,128]{1,0:T(8,128)} %bitcast.3, bf16[64,2048]{1,0:T(8,128)(2,1)} %frames_hbm.1), custom_call_target="tpu_custom_call" | custom-call | tf_op jit(solution)/shard_map/covariances/pallas_call | solution.py:464
  69.4 3.6 %decode.1 = (f32[2048,128]{1,0:T(8,128)}, f32[2048,128]{1,0:T(8,128)}) custom-call(s16[16,2,144,128]{3,2,1,0:T(8,128)(2,1)} %covariances.1.code_ref), custom_call_target="tpu_custom_call" | custom-call | tf_op jit(solution)/shard_map/decode/pallas_call | solution.py:500

commit v5 on v4

--- a/solution.py
+++ b/solution.py
@@ -151,7 +151,7 @@
         return remote(ref, ref, ring_s.at[d, s, h - 1], ring_r.at[d, s, h - 1], ahead_z(d))
 
     def ring_a1(q, d, h):
-        ref = row.at[q, behind(d, h - 1), :, LANES[A1]]
+        ref = row.at[pl.ds(2 * q, 2), behind(d, h - 1), :, LANES[A1]]
         return remote(ref, ref, a1_s.at[d, q, h - 1], a1_r.at[d, q, h - 1], ahead_z(d))
 
     def over_y(d, h):
@@ -163,7 +163,7 @@
         mean = rmean[lo:lo + 1, :]
         if s == B:
             mean = jnp.concatenate([mean, rmean[1:2, :]], axis=1)
-        for q in range(NX) if only is None else (only,):
+        for q in range(NX) if only is None else (2 * only, 2 * only + 1):
             base = (q * NZ + blk) * 2
             frames, inner = (at(base // 2, W), slice(None)) if half is None else (at(base + half, 64), at(half, 64))
             v = row[q, blk, inner, LANES[s]].astype(jnp.float32)
@@ -193,10 +193,10 @@
                 center_rows(B, behind(d, h), 1 - yl)
 
     def a1_goes(q, d, h):
-        return h < 4 or q // 2 == d
+        return h < 4 or q == d
 
     def a1_step(h):
-        for q in range(NX):
+        for q in range(2):
             for d in (0, 1):
                 if a1_goes(q, d, h):
                     ring_a1(q, d, h).wait_recv()
@@ -204,7 +204,7 @@
                         ring_a1(q, d, h + 1).start()
 
     def center_a1(h):
-        for q in range(NX):
+        for q in range(2):
             for d in (0, 1):
                 if a1_goes(q, d, h):
                     center_rows(A1, behind(d, h), only=q)
@@ -233,6 +233,8 @@
             if which == d:
                 col_forward(d).start()
             col_c(which, NX - 1 if d == 0 else 1).start()
+
+    def center_x(which):
         for k in (NX - 1, 1):
             center_columns(other_tile if which else tile, (x + k) % NX)
 
@@ -355,70 +357,72 @@
 
     ring_step(B, 1)
     ring_step(A0, 1)
+    for q in (0, 1):
+        for d in (0, 1):
+            ring_a1(q, d, 1).start()
+    col_y().wait_recv()
+    for d in (0, 1):
+        col_x(d, 1).start()
+    col_c(1, 0).start()
+    col_step_x(0)
+    ring_step(B, 2)
     for cp in row_parts:
         cp.wait_recv()
     rmean[...] = jnp.sum(rsum[...].reshape(NZ * NL, 8, W), axis=0) / total
     center_rows(B, z, yl)
+    center_step(B, 1)
     center_rows(A0, z)
-    center_rows(A1, z)
-    col_y().wait_recv()
-    for d in (0, 1):
-        col_x(d, 1).start()
-    col_c(1, 0).start()
-    ring_step(B, 2)
-    center_step(B, 1)
+    center_step(A0, 1)
+    ring_step(A0, 2)
     for cp in col_parts:
         cp.wait_recv()
     cmean[...] = (csum[:, 0] + csum[:, 1] + csum[:, 2] + csum[:, 3]) / total
-    center_step(A0, 1)
-    ring_step(A0, 2)
-    col_step_x(0)
     center_columns(tile, x)
+    col_step_x(1)
+    a1_step(1)
     center_columns(other_tile, x)
+    center_x(0)
+    center_rows(A1, z)
     center_step(B, 2)
     ring_step(B, 3)
-    for q in range(NX):
-        for d in (0, 1):
-            ring_a1(q, d, 1).start()
+    center_x(1)
     center_step(A0, 2)
+    for d in (0, 1):
+        col_forward(d).wait_recv()
+        col_c(d, 2).start()
+    ring_step(A0, 3)
+    for d in (0, 1):
+        center_columns(other_tile if d else tile, (x + 2) % NX)
+    center_a1(1)
     from_core(0, 0)
     from_core(1, 0)
+    from_core(0, 1)
+    from_core(0, 3)
     from_y(0)
     from_y(1)
-    ring_step(A0, 3)
-    col_step_x(1)
     center_step(B, 3)
     center_step(A0, 3)
-    from_core(0, 1)
-    from_core(0, 3)
+    a1_step(2)
+    center_a1(2)
+    from_core(1, 1)
+    from_core(1, 3)
+    from_y(2)
     ring_step(B, 4)
     ring_step(A0, 4)
     center_step(B, 4)
     center_step(A0, 4)
-    from_y(2)
-    for d in (0, 1):
-        col_forward(d).wait_recv()
-        col_c(d, 2).start()
-    for d in (0, 1):
-        center_columns(other_tile if d else tile, (x + 2) % NX)
-    a1_step(1)
-    from_core(1, 1)
-    from_core(1, 3)
     from_core(0, 2)
     from_core(1, 2)
     multiply(A0, 0)
-    a1_step(2)
-    center_a1(1)
+    a1_step(3)
     from_y(3)
     from_y(4)
     multiply(B, 0)
-    a1_step(3)
     lagged_columns(0, 32)
-    center_a1(2)
+    center_a1(3)
     multiply(A0, 1)
-    center_a1(3)
+    multiply(B, 1)
     a1_step(4)
-    multiply(B, 1)
     center_a1(4)
     multiply(A1, 0)
     multiply(A1, 1)
@@ -429,7 +433,7 @@
         for s in (B, A0):
             for h in range(1, HOPS[s][d] + 1):
                 ring(s, d, h).wait_send()
-        for q in range(NX):
+        for q in range(2):
             for h in range(1, 5):
                 if a1_goes(q, d, h):
                     ring_a1(q, d, h).wait_send()
@@ -485,7 +489,7 @@
             pltpu.VMEM((8, W), jnp.float32),
             pltpu.VMEM((4, 8, W), jnp.float32),
             dma((3,)), dma((2,)), dma((4,)), dma((4,)), dma((8,)), dma((8,)), dma((16,)), dma((16,)),
-            dma((2, 2, 4)), dma((2, 2, 4)), dma((2, NX, 4)), dma((2, NX, 4)), dma((2, 5)), dma((2, 5)),
+            dma((2, 2, 4)), dma((2, 2, 4)), dma((2, 2, 4)), dma((2, 2, 4)), dma((2, 5)), dma((2, 5)),
             dma((NZ, NL)), dma((NZ, NL)), dma((NX, 4)), dma((NX, 4)),
             dma(()), dma(()), dma((2, 2)), dma((2, 2)), dma((2,)), dma((2,)), dma((2, 4)), dma((2, 4)),
             dma((4, 2, NX)), dma((4, 2, NX)), dma((4, 2)),
@@ -494,7 +498,7 @@
             collective_id=0, has_side_effects=True, vmem_limit_bytes=56 << 20),
         name="covariances",
     )(partner.reshape(BLOCKS, W), usable.reshape(BLOCKS, W), frames)
-    step = blocks // 4
+    step = blocks // 2
     result = jax.ShapeDtypeStruct((blocks * W, W), jnp.float32)
     spec = pl.BlockSpec((step * W, W), lambda i: (i, 0))
     return pl.pallas_call(

time: 73.2 us -> 69.9 us (0.955)
  Pallas kernels: 72.4 us -> 68.6 us
    pallas_call x1, Pallas kernels: 68.8 us -> 66.1 us  [shards(): pl.pallas_call(kernel, out_shape=out, in_specs=[anywhere] * 3, out_specs=...]
    pallas_call x1, Pallas kernels: 3.64 us -> 2.49 us  [shards(): pl.pallas_call(decode, grid=(blocks // step,), out_shape=(result, result)...]
where the time goes in v5:
time: 69.9 us; the launch traced here: 69.3 us
  Pallas kernels  68.6 us (98%)
    pallas_call x1, Pallas kernels, shards(): pl.pallas_call(kernel, out_shape=out, in_specs=[anywhere] * 3, out_specs=...  66.1 us
    pallas_call x1, Pallas kernels, shards(): pl.pallas_call(decode, grid=(blocks // step,), out_shape=(result, result)...  2.49 us

profile of v5, /device:TPU:1, one launch (start us, length us, event | category | flops | bytes accessed | tf_op | source)
XLA Modules:
  0.0 69.3 jit_solution(17792485934583368602)
XLA Ops:
  0.6 66.1 %covariances.1.code_ref = s16[16,2,144,128]{3,2,1,0:T(8,128)(2,1)} custom-call(s32[32,128]{1,0:T(8,128)} %bitcast.2, s32[32,128]{1,0:T(8,128)} %bitcast.3, bf16[64,2048]{1,0:T(8,128)(2,1)} %frames_hbm.1), custom_call_target="tpu_custom_call" | custom-call | tf_op jit(solution)/shard_map/covariances/pallas_call | solution.py:468
  66.8 2.5 %decode.1 = (f32[2048,128]{1,0:T(8,128)}, f32[2048,128]{1,0:T(8,128)}) custom-call(s16[16,2,144,128]{3,2,1,0:T(8,128)(2,1)} %covariances.1.code_ref), custom_call_target="tpu_custom_call" | custom-call | tf_op jit(solution)/shard_map/decode/pallas_call | solution.py:504

commit v6 on v5

--- a/solution.py
+++ b/solution.py
@@ -298,14 +298,15 @@
             ul[frames, at(t, W)] = (v - now).astype(jnp.bfloat16)
             vl[frames, at(t, W)] = (v - lag).astype(jnp.bfloat16)
 
-    def lagged_columns(lo, hi):
-        def body(i, _):
+    def lagged_columns(xs):
+        def body(k, _):
+            i = xs * 8 + k
             v = vl[pl.ds(pl.multiple_of(i * W, W), 2 * W), :]
             lagged = jnp.dot(pick[at(i, W), :], v, preferred_element_type=jnp.float32)
             ul[at(i, W), pl.ds(512, 512)] = lagged.astype(jnp.bfloat16)
             return 0
 
-        lax.fori_loop(lo, hi, body, 0, unroll=4)
+        lax.fori_loop(0, 8, body, 0, unroll=4)
 
     def out_copy(j, w, dx):
         tx = (x + dx) % NX
@@ -411,6 +412,8 @@
     ring_step(A0, 4)
     center_step(B, 4)
     center_step(A0, 4)
+    lagged_columns((x + 3) % NX)
+    lagged_columns(x)
     from_core(0, 2)
     from_core(1, 2)
     multiply(A0, 0)
@@ -418,7 +421,8 @@
     from_y(3)
     from_y(4)
     multiply(B, 0)
-    lagged_columns(0, 32)
+    lagged_columns((x + 1) % NX)
+    lagged_columns((x + 2) % NX)
     center_a1(3)
     multiply(A0, 1)
     multiply(B, 1)

time: 69.9 us -> 69.4 us (level)
  no operation moved by 1% of the time
where the time goes in v6:
time: 69.4 us; the launch traced here: 68.9 us
  Pallas kernels  68.2 us (98%)
    pallas_call x1, Pallas kernels, shards(): pl.pallas_call(kernel, out_shape=out, in_specs=[anywhere] * 3, out_specs=...  65.7 us
    pallas_call x1, Pallas kernels, shards(): pl.pallas_call(decode, grid=(blocks // step,), out_shape=(result, result)...  2.49 us

profile of v6, /device:TPU:1, one launch (start us, length us, event | category | flops | bytes accessed | tf_op | source)
XLA Modules:
  0.0 68.9 jit_solution(11471575969479298525)
XLA Ops:
  0.6 65.7 %covariances.1.code_ref = s16[16,2,144,128]{3,2,1,0:T(8,128)(2,1)} custom-call(s32[32,128]{1,0:T(8,128)} %bitcast.2, s32[32,128]{1,0:T(8,128)} %bitcast.3, bf16[64,2048]{1,0:T(8,128)(2,1)} %frames_hbm.1), custom_call_target="tpu_custom_call" | custom-call | tf_op jit(solution)/shard_map/covariances/pallas_call | solution.py:472
  66.4 2.5 %decode.1 = (f32[2048,128]{1,0:T(8,128)}, f32[2048,128]{1,0:T(8,128)}) custom-call(s16[16,2,144,128]{3,2,1,0:T(8,128)(2,1)} %covariances.1.code_ref), custom_call_target="tpu_custom_call" | custom-call | tf_op jit(solution)/shard_map/decode/pallas_call | solution.py:508
